TPU v7x, 32 devices: a whole 2x2x4 slice. The times are simulated.
32 devices in a mesh: ens: 2 (over y), lon: 4 (over z), lat: 4 (over x, core).
Axes of the slice: x: 2, y: 2, z: 4, core: 2. Of those that a mesh axis runs over, the one named last changes fastest.
Arguments:
- field: float32 [8, 1440, 640], P(('ens', 'lat'), 'lon'), parts along dimension 0, may hold values from -6 to 6
- piece_lengths: int32 [4], replicated, may hold values from 1 to 360, 720 in all
- offsets: int32 [4], replicated, may hold values from 0 to 2, as said below
- basis: float32 [9, 4, 2, 17], replicated, may hold values from -1 to 1
- depth_weight: float32 [9, 640], replicated, may hold values from -2 to 2
- gain: float32 [640], replicated, may hold values from 0.5 to 1.5
- w_in: bfloat16 [640, 1280], replicated, may hold values from -0.25 to 0.25
- b_in: float32 [1280], replicated, may hold values from -3 to 3
- w_out: bfloat16 [1280, 640], replicated, may hold values from -0.15625 to 0.15625
- b_out: float32 [640], replicated, may hold values from -3 to 3
Outputs:
- result: float32 [8, 1440, 640], P(('ens', 'lat'), 'lon'), parts along dimension 0
There are 2 independent parts, one for each index of `ens`. A program takes and returns all parts, laid end to end along the dimension named above; an argument that names none is the same for every part. Nothing has to cross between parts.
Inputs may be any that keep to these rules, and one draw needn't show every extreme that they name: Index b of lon holds longitudes starts[b] to starts[b] + piece_lengths[b] - 1 in its first piece_lengths[b] slots; the lengths sum to 720. Output row i reads latitude rows offsets[i] to offsets[i] + 1, and i - 1 <= offsets[i] <= i.
All inputs are finite; a program needn't handle non-finite values.
Results may differ from a plain program's by a relative error of at most 0.0018.
Values sent between devices are 32-bit elements; how exact they have to be, the bound alone decides.
No kernel may reach another device: no remote copies, remote signals or barrier semaphores. Data moves between devices by JAX's collectives and lax.ppermute only.
A program may use at most 64 MiB of HBM per device.

v0:
```python
import jax
import jax.numpy as jnp
from jax import lax
from jax.sharding import PartitionSpec as P

NLON = 720


def from_behind(value, axis, steps):
    count = lax.axis_size(axis)
    initial, last = (max(0, -steps), min(count, count - steps))
    return lax.ppermute(value, axis, [(source, source + steps) for source in range(initial, last)])


def on_device(field, piece_lengths, offsets, basis, depth_weight, gain, w_in, b_in, w_out, b_out):
    rows_dev, slot_cap, channels = field.shape
    groups = lax.axis_size("lon")
    lon_index = lax.axis_index("lon")
    lat_index = lax.axis_index("lat")
    lat_rows = basis.shape[1]
    support = basis.shape[2]
    lon_taps = basis.shape[3]
    half_taps = lon_taps // 2
    chan_group = channels // groups
    starts = jnp.cumsum(piece_lengths) - piece_lengths
    group_ids = jnp.arange(groups, dtype=jnp.int32)
    longitudes = jnp.arange(NLON, dtype=jnp.int32)
    owner = jnp.sum((starts[None, :] <= longitudes[:, None]).astype(jnp.int32), axis=1) - 1
    own_start = jnp.sum(jnp.where(group_ids[None, :] == owner[:, None], starts[None, :], 0), axis=1)
    slot_index = owner * slot_cap + longitudes - own_start
    slot_pos = jnp.arange(groups * slot_cap, dtype=jnp.int32)
    slot_owner = slot_pos // slot_cap
    slot_within = slot_pos % slot_cap
    owner_match = slot_owner[:, None] == group_ids[None, :]
    owner_length = jnp.sum(jnp.where(owner_match, piece_lengths[None, :], 0), axis=1)
    owner_start = jnp.sum(jnp.where(owner_match, starts[None, :], 0), axis=1)
    slot_valid = (slot_within < owner_length).astype(jnp.float32)
    dense_of_slot = jnp.clip(owner_start + slot_within, 0, NLON - 1)
    by_channel = jnp.transpose(field, (0, 2, 1))
    dense = jnp.take(
        lax.all_to_all(by_channel, "lon", split_axis=1, concat_axis=2, tiled=True),
        slot_index,
        axis=2,
    )
    chan_weight = lax.dynamic_slice_in_dim(depth_weight, lon_index * chan_group, chan_group, 1)
    coefficients = jnp.einsum("kism,kc->ismc", basis, chan_weight, precision=lax.Precision.HIGHEST)
    first_row = lat_index * rows_dev
    reach_dev = min(lax.axis_size("lat") - 1, (support + rows_dev - 2) // rows_dev)

    def contribution(out_start, taps_in, in_first):
        count_in = taps_in.shape[1]
        coef_rows = lax.dynamic_slice_in_dim(coefficients, out_start, rows_dev, 0)
        off_rows = lax.dynamic_slice_in_dim(offsets, out_start, rows_dev, 0)
        one_hot = (
            off_rows[:, None, None] + jnp.arange(support, dtype=jnp.int32)[None, :, None]
            == in_first + jnp.arange(count_in, dtype=jnp.int32)[None, None, :]
        ).astype(jnp.float32)
        mixing = jnp.einsum("isj,ismc->ijmc", one_hot, coef_rows, precision=lax.Precision.HIGHEST)
        return jnp.einsum("ijmc,mjcl->icl", mixing, taps_in, precision=lax.Precision.HIGHEST)

    own_taps = jnp.stack([jnp.roll(dense, half_taps - tap, axis=2) for tap in range(lon_taps)], 0)
    conv = contribution(first_row, own_taps, first_row)
    for offset_dev in range(-reach_dev, reach_dev + 1):
        if offset_dev != 0:
            target = jnp.clip((lat_index + offset_dev) * rows_dev, 0, lat_rows - rows_dev)
            term = contribution(target, own_taps, first_row)
            conv = conv + from_behind(term, "lat", offset_dev)
    to_slots = jnp.take(conv, dense_of_slot, axis=2) * slot_valid[None, None, :]
    merged = lax.all_to_all(to_slots, "lon", split_axis=2, concat_axis=1, tiled=True)
    conv_slots = jnp.transpose(merged, (0, 2, 1))
    state = field + conv_slots
    mean_sq = jnp.mean(state * state, axis=-1, keepdims=True)
    normed = (state * lax.rsqrt(mean_sq + 1e-05) * gain).astype(jnp.bfloat16).reshape(-1, channels)
    pre = jnp.dot(normed, w_in, preferred_element_type=jnp.float32) + b_in
    activated = jax.nn.gelu(pre, approximate=False).astype(jnp.bfloat16)
    mlp_out = jnp.dot(activated, w_out, preferred_element_type=jnp.float32) + b_out
    output = state + mlp_out.reshape(rows_dev, slot_cap, channels)
    own_length = jnp.sum(jnp.where(group_ids == lon_index, piece_lengths, 0))
    local_valid = (jnp.arange(slot_cap, dtype=jnp.int32) < own_length).astype(jnp.float32)
    return output * local_valid[None, :, None]


def solution(mesh):
    placed = (P(("ens", "lat"), "lon", None), P(), P(), P(), P(), P(), P(), P(), P(), P())
    return jax.shard_map(
        on_device,
        mesh=mesh,
        in_specs=placed,
        out_specs=P(("ens", "lat"), "lon", None),
        check_vma=False,
    )
```

profile of v0, /device:TPU:0, one launch (start us, length us, event | category | flops | bytes accessed | tf_op | source)
XLA Modules:
  0.0 123.4 jit_solution(5536487936589261706)
XLA Ops:
  0.0 3.3 %copy.35 = f32[1,360,640]{1,0,2:T(1,128)} copy(f32[1,360,640]{2,1,0:T(8,128)} %param.10) | data formatting | bytes 1843200 | tf_op args[0]
  3.3 6.4 %all-to-all-start = ((f32[1,640,360]{2,0,1:T(1,128)}), f32[1,640,360]{2,0,1:T(1,128)S(1)}, u32[]{:S(2)}, u32[]{:S(2)}) async-start(f32[1,640,360]{2,0,1:T(1,128)} %bitcast.197), calls=%async_computation | async-start | bytes 1966080 | tf_op jit(solution)/shard_map/all_to_all | solution.py:41
  9.7 0.2 reduce-window.9
  9.9 0.7 bitcast_subtract_fusion
  10.5 1.1 fusion.74
  11.7 0.6 fusion.159
  12.3 0.8 fusion.80
  13.1 0.1 convert_reduce_fusion
  13.2 0.1 select_reduce_fusion.2
  13.4 0.8 fusion.76
  14.2 0.8 fusion.78
  15.1 19.0 %all-to-all-done = f32[1,640,360]{2,0,1:T(1,128)S(1)} async-done(((f32[1,640,360]{2,0,1:T(1,128)}), f32[1,640,360]{2,0,1:T(1,128)S(1)}, u32[]{:S(2)}, u32[]{:S(2)}) %all-to-all-start) | async-done | bytes 921632 | tf_op jit(solution)/shard_map/all_to_all | solution.py:41
  34.0 1.0 copy.74
  35.0 1.7 %copy.36 = f32[1,160,4,360]{1,3,2,0:T(8,128)S(1)} copy(f32[1,160,4,360]{3,1,2,0:T(8,128)} %bitcast.196) | data formatting | bytes 1843200 | tf_op jit(solution)/shard_map/all_to_all | solution.py:41
  36.7 2.9 %gather_fusion = f32[720,160]{1,0:T(8,128)} fusion(f32[160,1440]{0,1:T(8,128)S(1)} %bitcast.194, s32[1024]{0:T(1024)S(1)} %pad_clamp_fusion.1), kind=kCustom, calls=%fused_computation | custom fusion | bytes 924480 | tf_op jit(solution)/shard_map/jit(_take)/gather | solution.py:40
  39.6 1.3 %bitcast_select_fusion.2 = f32[1,160,720]{1,2,0:T(8,128)S(1)} fusion(f32[720,160]{1,0:T(8,128)} %gather_fusion, pred[720]{0:T(1024)(128)(4,1)S(1)} %compare_and_fusion.1), kind=kLoop, calls=%fused_computation.102 | loop fusion | flops 115200 | bytes 922320 | tf_op jit(solution)/shard_map/jit(_take)/select_n | solution.py:40
  40.9 0.1 fusion.143
  41.0 0.1 fusion.145
  41.1 0.1 fusion.147
  41.3 0.1 fusion.149
  41.4 0.1 fusion.151
  41.5 0.1 fusion.153
  41.7 0.1 fusion.155
  41.8 0.1 fusion.157
  41.9 0.1 fusion.48
  42.0 0.1 fusion.49
  42.1 0.1 fusion.50
  42.1 0.1 fusion.51
  42.2 0.1 fusion.52
  42.3 0.1 fusion.53
  42.4 0.0 copy-start.1
  42.4 0.1 fusion.54
  42.4 0.1 fusion.55
  42.5 1.0 copy-done.1
  43.5 0.2 fusion.64
  43.6 0.1 fusion.56
  43.7 0.1 fusion.57
  43.8 0.1 fusion.58
  43.8 0.1 fusion.59
  43.9 0.1 fusion.60
  43.9 0.1 fusion.61
  44.0 0.1 fusion.62
  44.1 0.1 fusion.63
  44.1 4.3 %fusion = (f32[160,720]{0,1:T(8,128)}, f32[160,720]{0,1:T(8,128)S(1)}, f32[160,720]{0,1:T(8,128)S(1)}) fusion(f32[17,1,160,720]{2,3,1,0:T(8,128)S(1)} %fusion.63, f32[160,17]{0,1:T(8,128)S(1)} %bitcast.201, f32[160,17]{0,1:T(8,128)S(1)} %get-tuple-element.53, f32[160,17]{0,1:T(8,128)S(1)} %get-tuple-element.52), kind=kLoop, calls=%fused_computation.5 | loop fusion | flops 11404800 | bytes 9248640 | tf_op jit(solution)/shard_map/ijmc,mjcl->icl/dot_general | solution.py:59
  48.5 1.0 copy.61
  49.5 1.3 %collective-permute-start = (f32[1,160,720]{2,1,0:T(8,128)}, f32[1,160,720]{2,1,0:T(8,128)}, u32[]{:S(2)}, u32[]{:S(2)}) collective-permute-start(f32[1,160,720]{2,1,0:T(8,128)} %bitcast.199), channel_id=1, source_target_pairs={{1,0},{2,1},{3,2},{5,4},{6,5},{7,6},{9,8},{10,9},{11,10},{13,12},{... | collective-permute-start | bytes 1382408 | tf_op jit(solution)/shard_map/ppermute | solution.py:12
  50.8 1.0 copy.70
  51.8 3.0 %collective-permute-start.1 = (f32[1,160,720]{2,1,0:T(8,128)}, f32[1,160,720]{2,1,0:T(8,128)S(1)}, u32[]{:S(2)}, u32[]{:S(2)}) collective-permute-start(f32[1,160,720]{2,1,0:T(8,128)} %bitcast.200), channel_id=1, source_target_pairs={{0,1},{1,2},{2,3},{4,5},{5,6},{6,7},{8,9},{9,10},{10,11},{12,13},{... | collective-permute-start | bytes 1382408 | tf_op jit(solution)/shard_map/ppermute | solution.py:12
  54.9 0.1 select_reduce_fusion
  55.0 0.1 fusion.96
  55.1 2.2 %copy.38 = f32[1,160,720]{1,2,0:T(8,128)} copy(f32[1,160,720]{2,1,0:T(8,128)} %collective-permute-done) | data formatting | bytes 921600 | tf_op jit(solution)/shard_map/ppermute | solution.py:12
  57.3 1.1 copy.39
  58.4 1.5 %fusion.66 = f32[160,720]{0,1:T(8,128)S(1)} fusion(f32[1,160,720]{1,2,0:T(8,128)} %copy.39, f32[1,160,720]{1,2,0:T(8,128)} %copy.38, f32[160,720]{0,1:T(8,128)S(1)} %copy-done.3), kind=kLoop, calls=%fused_computation.105 | loop fusion | flops 230400 | bytes 1843200 | tf_op jit(solution)/shard_map/add | solution.py:67
  59.9 4.6 %gather_fusion.1 = f32[1440,160]{1,0:T(8,128)} fusion(f32[160,720]{0,1:T(8,128)S(1)} %fusion.66, s32[2048]{0:T(1024)S(1)} %pad_clamp_fusion), kind=kCustom, calls=%fused_computation.1 | custom fusion | bytes 1848960 | tf_op jit(solution)/shard_map/jit(_take)/gather | solution.py:68
  64.5 1.8 %copy.40 = f32[1440,160]{0,1:T(8,128)S(1)} copy(f32[1440,160]{1,0:T(8,128)} %gather_fusion.1) | data formatting | bytes 1843200 | tf_op jit(solution)/shard_map/jit(_take)/gather | solution.py:68
  66.3 1.1 fusion.16
  67.4 4.7 %copy.41 = f32[1,160,1440]{1,0,2:T(1,128)} copy(f32[1,160,1440]{2,1,0:T(8,128)} %fusion.16) | data formatting | bytes 1843200 | tf_op jit(solution)/shard_map/mul | solution.py:68
  72.1 3.7 %all-to-all-start.1 = ((f32[1,160,1440]{1,0,2:T(1,128)}), f32[1,160,1440]{1,0,2:T(1,128)S(1)}, u32[]{:S(2)}, u32[]{:S(2)}) async-start(f32[1,160,1440]{1,0,2:T(1,128)} %copy.41), calls=%async_computation.1 | async-start | bytes 2949120 | tf_op jit(solution)/shard_map/all_to_all | solution.py:69
  75.8 0.6 fusion.98
  76.4 34.4 %all-to-all-done.1 = f32[1,160,1440]{1,0,2:T(1,128)S(1)} async-done(((f32[1,160,1440]{1,0,2:T(1,128)}), f32[1,160,1440]{1,0,2:T(1,128)S(1)}, u32[]{:S(2)}, u32[]{:S(2)}) %all-to-all-start.1) | async-done | bytes 921632 | tf_op jit(solution)/shard_map/all_to_all | solution.py:69
  110.8 3.1 %copy.42 = f32[1,160,4,360]{3,1,2,0:T(8,128)} copy(f32[1,160,4,360]{1,0,3,2:T(1,128)S(1)} %bitcast.195) | data formatting | bytes 1843200 | tf_op jit(solution)/shard_map/all_to_all | solution.py:69
  114.0 1.6 %copy.43 = f32[1,640,360]{1,2,0:T(8,128)S(1)} copy(f32[1,640,360]{2,1,0:T(8,128)} %bitcast.198) | data formatting | bytes 1843200 | tf_op jit(solution)/shard_map/all_to_all | solution.py:69
  115.6 0.2 multiply_reduce_fusion
  115.8 7.6 %fusion.15 = f32[1,360,640]{2,1,0:T(8,128)} fusion(bf16[1280,640]{1,0:T(8,128)(2,1)S(1)} %copy-done, bf16[640,1280]{1,0:T(8,128)(2,1)} %param.16, f32[1280]{0:T(1024)S(1)} %copy-done.7, f32[360]{0:T(512)S(1)} %fusion.98, f32[640]{0:T(1024)S(1)} %copy-done.8, f32[640]{0:T(1024)S(1)} %copy-done.9, f32[360]{0:T(512)S(1)} %add_rsqrt_fusion, ...), kind=kOutput, calls=%fused_computation.31 | convolution fusion | flops 1211904000 | bytes 6054720 | tf_op jit(solution)/shard_map/dot_general | solution.py:76
  (39 shorter events, 0.2 us)
Async XLA Ops:
  0.0 115.8 %copy-start = (bf16[1280,640]{1,0:T(8,128)(2,1)S(1)}, bf16[1280,640]{1,0:T(8,128)(2,1)}, u32[]{:S(2)}) copy-start(bf16[1280,640]{1,0:T(8,128)(2,1)} %param.18) | copy-start | bytes 4915204
  0.0 9.7 %copy-start.6 = (s32[4]{0:T(128)S(1)}, s32[4]{0:T(128)}, u32[]{:S(2)}) copy-start(s32[4]{0:T(128)} %param.11) | copy-start | bytes 52
  0.0 10.5 %copy-start.4 = (f32[9,4,2,17]{3,2,1,0:T(2,128)S(1)}, f32[9,4,2,17]{3,2,1,0:T(2,128)}, u32[]{:S(2)}) copy-start(f32[9,4,2,17]{3,2,1,0:T(2,128)} %param.13) | copy-start | bytes 14692
  0.0 11.7 %copy-start.5 = (s32[4]{0:T(128)S(1)}, s32[4]{0:T(128)}, u32[]{:S(2)}) copy-start(s32[4]{0:T(128)} %param.12) | copy-start | bytes 52
  3.3 30.7 %all-to-all-start = ((f32[1,640,360]{2,0,1:T(1,128)}), f32[1,640,360]{2,0,1:T(1,128)S(1)}, u32[]{:S(2)}, u32[]{:S(2)}) async-start(f32[1,640,360]{2,0,1:T(1,128)} %bitcast.197), calls=%async_computation | async-start | bytes 1966080 | tf_op jit(solution)/shard_map/all_to_all | solution.py:41
  42.4 1.1 copy-start.1
  49.5 5.6 %collective-permute-start = (f32[1,160,720]{2,1,0:T(8,128)}, f32[1,160,720]{2,1,0:T(8,128)}, u32[]{:S(2)}, u32[]{:S(2)}) collective-permute-start(f32[1,160,720]{2,1,0:T(8,128)} %bitcast.199), channel_id=1, source_target_pairs={{1,0},{2,1},{3,2},{5,4},{6,5},{7,6},{9,8},{10,9},{11,10},{13,12},{... | collective-permute-start | bytes 1382408 | tf_op jit(solution)/shard_map/ppermute | solution.py:12
  50.8 7.6 %copy-start.3 = (f32[160,720]{0,1:T(8,128)S(1)}, f32[160,720]{0,1:T(8,128)}, u32[]{:S(2)}) copy-start(f32[160,720]{0,1:T(8,128)} %get-tuple-element.5) | copy-start | bytes 1382404
  51.8 5.4 %collective-permute-start.1 = (f32[1,160,720]{2,1,0:T(8,128)}, f32[1,160,720]{2,1,0:T(8,128)S(1)}, u32[]{:S(2)}, u32[]{:S(2)}) collective-permute-start(f32[1,160,720]{2,1,0:T(8,128)} %bitcast.200), channel_id=1, source_target_pairs={{0,1},{1,2},{2,3},{4,5},{5,6},{6,7},{8,9},{9,10},{10,11},{12,13},{... | collective-permute-start | bytes 1382408 | tf_op jit(solution)/shard_map/ppermute | solution.py:12
  72.1 38.8 %all-to-all-start.1 = ((f32[1,160,1440]{1,0,2:T(1,128)}), f32[1,160,1440]{1,0,2:T(1,128)S(1)}, u32[]{:S(2)}, u32[]{:S(2)}) async-start(f32[1,160,1440]{1,0,2:T(1,128)} %copy.41), calls=%async_computation.1 | async-start | bytes 2949120 | tf_op jit(solution)/shard_map/all_to_all | solution.py:69
  114.0 1.6 %copy-start.2 = (f32[1,360,640]{2,1,0:T(8,128)S(1)}, f32[1,360,640]{2,1,0:T(8,128)}, u32[]{:S(2)}) copy-start(f32[1,360,640]{2,1,0:T(8,128)} %param.10) | copy-start | bytes 2764804
  114.0 1.8 %copy-start.7 = (f32[1280]{0:T(1024)S(1)}, f32[1280]{0:T(1024)}, u32[]{:S(2)}) copy-start(f32[1280]{0:T(1024)} %param.17) | copy-start | bytes 15364
  114.0 1.8 %copy-start.8 = (f32[640]{0:T(1024)S(1)}, f32[640]{0:T(1024)}, u32[]{:S(2)}) copy-start(f32[640]{0:T(1024)} %param.19) | copy-start | bytes 7684
  114.0 1.8 %copy-start.9 = (f32[640]{0:T(1024)S(1)}, f32[640]{0:T(1024)}, u32[]{:S(2)}) copy-start(f32[640]{0:T(1024)} %param.15) | copy-start | bytes 7684
where the time goes:
time: 125 us; the launch traced here: 123 us
  waiting for transfers between devices  53.4 us (43%)
  local copies, waits for them, and re-layouts  32.7 us (26%)
  starting transfers between devices  14.4 us (12%)
  other arithmetic  11.3 us (9%)
  matrix products  11.1 us (9%)
    all_to_all x1, waiting for transfers between devices, on_device(): lax.all_to_all(to_slots, 'lon', split_axis=2, concat_axis=1, tiled=True)  34.4 us
    all_to_all x1, waiting for transfers between devices, on_device(): lax.all_to_all(by_channel, 'lon', split_axis=1, concat_axis=2, tiled=True)  19 us
    dot_general x1, matrix products, on_device(): jnp.dot(activated, w_out, preferred_element_type=jnp.float32) + b_out  7.57 us
    gather x2, local copies, waits for them, and re-layouts, on_device(): to_slots = jnp.take(conv, dense_of_slot, axis=2) * slot_valid[None, None, :]  6.43 us
    all_to_all x1, starting transfers between devices, on_device(): lax.all_to_all(by_channel, 'lon', split_axis=1, concat_axis=2, tiled=True)  6.35 us
    unnamed x24, local copies, waits for them, and re-layouts  5.37 us
    all_to_all x2, local copies, waits for them, and re-layouts, on_device(): lax.all_to_all(to_slots, 'lon', split_axis=2, concat_axis=1, tiled=True)  4.74 us
    mul x1, local copies, waits for them, and re-layouts, on_device(): to_slots = jnp.take(conv, dense_of_slot, axis=2) * slot_valid[None, None, :]  4.69 us
  transfers between devices with their start and end apart: 4, of which 2 were waited for; matrix products, arithmetic and copies ran while one was open for 8% of the time, Pallas kernels for 0%

commit v1 on v0

v1 whole, which is shorter than its diff:
```python
import functools

import jax
import jax.numpy as jnp
from jax import lax
from jax.experimental import pallas as pl
from jax.experimental.pallas import tpu as pltpu
from jax.sharding import PartitionSpec as P

LANES = 128
HBM = pl.BlockSpec(memory_space=pltpu.HBM)
SMEM = pl.BlockSpec(memory_space=pltpu.SMEM)
VMEM = pl.BlockSpec(memory_space=pltpu.VMEM)


def up8(value):
    return (value + 7) // 8 * 8


def in_vmem(value):
    return pltpu.with_memory_space_constraint(value, pltpu.VMEM)


def in_hbm(value):
    return pltpu.with_memory_space_constraint(value, pltpu.HBM)


def grant(mib):
    return pltpu.CompilerParams(vmem_limit_bytes=mib << 20)


def vmem_out(shape, dtype=jnp.float32):
    return pltpu.VMEM(shape, dtype)


def edges_kernel(half, lengths, own, out, rows, sems):
    length = lengths[lax.axis_index("lon")]
    cap = own.shape[0]
    last = jnp.maximum(length - half, 0)
    if cap % 8 == 0:
        base = pl.multiple_of(jnp.minimum(last // 8 * 8, cap - 16), 8)
        head = pltpu.make_async_copy(own.at[pl.ds(0, half), :], out.at[pl.ds(0, half), :], sems.at[0])
        tail = pltpu.make_async_copy(own.at[pl.ds(base, 16), :], rows.at[pl.ds(0, 16), :], sems.at[1])
        head.start()
        tail.start()
        head.wait()
        tail.wait()
        start = last - base
    else:
        whole = pltpu.make_async_copy(own, rows, sems.at[0])
        whole.start()
        whole.wait()
        out[pl.ds(0, half), :] = rows[pl.ds(0, half), :]
        start = last
    for near in range(half):
        out[pl.ds(half + near, 1), :] = rows[pl.ds(start + near, 1), :]


def halo_kernel(count, half, lengths, *refs):
    received, out, stack = refs[:-2], refs[-2], refs[-1]
    me = lax.axis_index("lon")
    for step, ref in enumerate(received):
        stack[pl.ds(step * 2 * half, 2 * half), :] = ref[...]

    def row_of(piece, row):
        behind = lax.rem(me - piece + count, count) - 1
        return behind * (2 * half) + row

    piece = lax.rem(me + count - 1, count)
    slot = lengths[piece] - 1
    for near in range(1, half + 1):
        row = half + slot - jnp.maximum(lengths[piece] - half, 0)
        out[pl.ds(half - near, 1), :] = stack[pl.ds(row_of(piece, row), 1), :]
        before = lax.rem(piece + count - 1, count)
        piece, slot = (
            jnp.where(slot > 0, piece, before),
            jnp.where(slot > 0, slot - 1, lengths[before] - 1),
        )
    piece = lax.rem(me + 1, count)
    slot = jnp.int32(0)
    for near in range(half):
        out[pl.ds(half + near, 1), :] = stack[pl.ds(row_of(piece, slot), 1), :]
        inside = slot + 1 < lengths[piece]
        piece, slot = (
            jnp.where(inside, piece, lax.rem(piece + 1, count)),
            jnp.where(inside, slot + 1, 0),
        )


def fill_window(window, rows, halos, half, length):
    cap = rows.shape[0]
    for column in range(window.shape[0]):
        lanes = pl.ds(column * LANES, LANES)
        window[column, pl.ds(0, half), :] = halos[pl.ds(0, half), lanes]
        window[column, pl.ds(half, cap), :] = rows[:, lanes]
    for column in range(window.shape[0]):
        lanes = pl.ds(column * LANES, LANES)
        window[column, pl.ds(half + length, half), :] = halos[pl.ds(half, half), lanes]


def add_taps(total, window, column, first, rows, coef, taps):
    lanes = pl.ds(column * LANES, LANES)
    for phase in range(min(8, taps)):
        steps = (taps - phase + 7) // 8
        block = window[column, pl.ds(first + phase, rows + 8 * (steps - 1)), :]
        for step in range(steps):
            weight = coef[pl.ds(8 * step + phase, 1), lanes]
            total = total + weight * block[8 * step : 8 * step + rows]
    return total


def own_kernel(half, block, lengths, offsets, basis, depth_weight, own_hbm, halos, *refs):
    held = (len(refs) - 6) // 2
    sources, out, coef_other, copied = refs[:held], refs[held], refs[held + 1], refs[held + 2 : 2 * held + 2]
    window, coef_own, own, sems = refs[2 * held + 2 :]
    own_copy = pltpu.make_async_copy(own_hbm, own, sems.at[0])
    own_copy.start()
    copies = [pltpu.make_async_copy(a, b, sems.at[1]) for a, b in zip(sources, copied)]
    for copy in copies:
        copy.start()
    lat = lax.axis_index("lat")
    length = lengths[lax.axis_index("lon")]
    at = lat - offsets[lat]
    taps = basis.shape[3]
    for which, ref in ((at, coef_own), (1 - at, coef_other)):
        ref[pl.ds(0, taps), :] = lax.dot_general(
            basis[:, lat, which, :],
            depth_weight[...],
            (((0,), (0,)), ((), ())),
            precision=lax.Precision.HIGHEST,
            preferred_element_type=jnp.float32,
        )
    own_copy.wait()
    fill_window(window, own, halos, half, length)
    rows_all = out.shape[0]
    for first in range(0, rows_all, block):
        rows = min(block, rows_all - first)
        for column in range(window.shape[0]):
            state = window[column, pl.ds(half + first, rows), :]
            out[pl.ds(first, rows), pl.ds(column * LANES, LANES)] = add_taps(
                state, window, column, first, rows, coef_own, taps
            )
    for copy in copies:
        copy.wait()


def block_kernel(half, taps, block, lengths, offsets, near, far, near_halo, far_halo, partial, coef, gain,
                 w_in, b_in, w_out, b_out, out, window, state, normed, hidden, result, sem):
    lat = lax.axis_index("lat")
    length = lengths[lax.axis_index("lon")]
    at = lat - offsets[lat]
    use_near = lax.rem(at + lat, 2) == 0
    columns = window.shape[0]
    width = columns * LANES
    cap = near.shape[0]

    @pl.when(use_near)
    def _():
        fill_window(window, near, near_halo, half, length)

    @pl.when(jnp.logical_not(use_near))
    def _():
        fill_window(window, far, far_halo, half, length)

    rows_all = partial.shape[0]
    copies = []
    for first in range(0, rows_all, block):
        rows = min(block, rows_all - first)
        here = pl.ds(first, rows)
        squares = jnp.zeros((rows, LANES), jnp.float32)
        for column in range(columns):
            lanes = pl.ds(column * LANES, LANES)
            value = add_taps(partial[here, lanes], window, column, first, rows, coef, taps)
            squares = squares + value * value
            state[pl.ds(0, rows), lanes] = value
        scale = lax.rsqrt(jnp.sum(squares, axis=1, keepdims=True) / width + 1e-05)
        normed[pl.ds(0, rows), :] = (state[pl.ds(0, rows), :] * scale * gain[...][None, :]).astype(jnp.bfloat16)
        step = 256
        for start in range(0, w_in.shape[1], step):
            part = pl.ds(start, step)
            pre = jnp.dot(normed[pl.ds(0, rows), :], w_in[:, part], preferred_element_type=jnp.float32)
            pre = pre + b_in[part][None, :]
            active = 0.5 * pre * (1.0 + lax.erf(pre * 0.7071067811865476))
            hidden[pl.ds(0, rows), part] = active.astype(jnp.bfloat16)
        inside = (lax.broadcasted_iota(jnp.int32, (rows, 1), 0) + first) < length
        mixed = jnp.dot(hidden[pl.ds(0, rows), :], w_out[...], preferred_element_type=jnp.float32)
        value = jnp.where(inside, state[pl.ds(0, rows), :] + (mixed + b_out[...][None, :]), 0.0)
        if cap % 8:
            kept = min(rows, cap - first)
            result[pl.ds(first, kept), :] = value[:kept]
        else:
            result[here, :] = value
            copy = pltpu.make_async_copy(result.at[here, :], out.at[here, :], sem)
            copy.start()
            copies.append(copy)
    if cap % 8:
        copy = pltpu.make_async_copy(result, out, sem)
        copy.start()
        copies.append(copy)
    for copy in copies:
        copy.wait()


def on_device(field, piece_lengths, offsets, basis, depth_weight, gain, w_in, b_in, w_out, b_out):
    _, cap, channels = field.shape
    count = lax.axis_size("lon")
    lats = lax.axis_size("lat")
    taps = basis.shape[3]
    half = taps // 2
    columns = channels // LANES
    cap8 = up8(cap)
    hid = w_in.shape[1]
    block = 120

    own = in_hbm(field.reshape(cap, channels))
    piece_lengths, offsets = in_hbm(piece_lengths), in_hbm(offsets)
    near_pairs = [(a, a ^ 1) for a in range(lats) if (a ^ 1) < lats]
    far_pairs = [(a, a + 1) for a in range(1, lats - 1, 2)] + [(a + 1, a) for a in range(1, lats - 1, 2)]

    def to_near(value):
        return lax.ppermute(value, "lat", near_pairs)

    def to_far(value):
        return lax.ppermute(value, "lat", far_pairs)

    far = to_far(own)
    near = to_near(own)
    edges = pl.pallas_call(
        functools.partial(edges_kernel, half),
        out_shape=vmem_out((2 * half, channels)),
        in_specs=[SMEM, HBM],
        out_specs=VMEM,
        scratch_shapes=[
            pltpu.VMEM((16 if cap % 8 == 0 else cap, channels), jnp.float32),
            pltpu.SemaphoreType.DMA((2,)),
        ],
        compiler_params=grant(8),
        name="edges",
    )(piece_lengths, own)
    received = [
        lax.ppermute(edges, "lon", [(p, (p + step) % count) for p in range(count)]) for step in range(1, count)
    ]
    halos = pl.pallas_call(
        functools.partial(halo_kernel, count, half),
        out_shape=vmem_out((2 * half, channels)),
        in_specs=[SMEM] + [VMEM] * len(received),
        out_specs=VMEM,
        scratch_shapes=[pltpu.VMEM((max(1, count - 1) * 2 * half, channels), jnp.float32)],
        compiler_params=grant(8),
        name="halo",
    )(piece_lengths, *[in_vmem(r) for r in received])
    near_halo, far_halo = to_near(halos), to_far(halos)
    window = pltpu.VMEM((columns, cap8 + 2 * half + 16, LANES), jnp.float32)
    operands = (gain, w_in, b_in, w_out, b_out)
    partial, coef, *operands = pl.pallas_call(
        functools.partial(own_kernel, half, block),
        out_shape=(
            vmem_out((cap8, channels)),
            vmem_out((up8(taps), channels)),
            *[vmem_out(value.shape, value.dtype) for value in operands],
        ),
        in_specs=[SMEM, SMEM, VMEM, VMEM, HBM, VMEM] + [HBM] * len(operands),
        out_specs=(VMEM,) * (2 + len(operands)),
        scratch_shapes=[
            window,
            pltpu.VMEM((up8(taps), channels), jnp.float32),
            pltpu.VMEM((cap, channels), jnp.float32),
            pltpu.SemaphoreType.DMA((2,)),
        ],
        compiler_params=grant(16),
        name="own",
    )(piece_lengths, offsets, in_hbm(basis), in_hbm(depth_weight), own, halos, *[in_hbm(v) for v in operands])
    most = min(block, cap8)
    out = pl.pallas_call(
        functools.partial(block_kernel, half, taps, block),
        out_shape=jax.ShapeDtypeStruct((cap, channels), jnp.float32),
        in_specs=[SMEM, SMEM] + [VMEM] * 11,
        out_specs=HBM,
        scratch_shapes=[
            window,
            pltpu.VMEM((most, channels), jnp.float32),
            pltpu.VMEM((most, channels), jnp.bfloat16),
            pltpu.VMEM((most, hid), jnp.bfloat16),
            pltpu.VMEM((cap, channels), jnp.float32),
            pltpu.SemaphoreType.DMA,
        ],
        compiler_params=grant(24),
        name="block",
    )(piece_lengths, offsets, in_vmem(near), in_vmem(far), in_vmem(near_halo), in_vmem(far_halo), partial, coef,
      *operands)
    return out.reshape(1, cap, channels)


def solution(mesh):
    placed = (P(("ens", "lat"), "lon", None), P(), P(), P(), P(), P(), P(), P(), P(), P())
    return jax.shard_map(
        on_device,
        mesh=mesh,
        in_specs=placed,
        out_specs=P(("ens", "lat"), "lon", None),
        check_vma=False,
    )
```

time: 125 us -> 27.3 us (0.22); the launches traced: 123 us -> 27 us
  waiting for transfers between devices: 53.4 us -> 4.8 us
  local copies, waits for them, and re-layouts: 32.7 us -> 0 us
  other arithmetic: 11.3 us -> 0 us
  matrix products: 11.1 us -> 0 us
  Pallas kernels: 0 us -> 10.5 us
  starting transfers between devices: 14.4 us -> 11.7 us
    all_to_all x2 -> x0, waiting for transfers between devices: 53.4 us -> none  [the longest x1 34.4 us: on_device(): lax.all_to_all(to_slots, 'lon', split_axis=2, concat_axis=1, tiled=True)]
    dot_general x5 -> x0, matrix products: 11.1 us -> none  [the longest x1 7.57 us: on_device(): jnp.dot(activated, w_out, preferred_element_type=jnp.float32) + b_out]
    pallas_call x0 -> x4, Pallas kernels: none -> 10.5 us  [the longest x1 4.98 us: on_device(): pl.pallas_call(functools.partial(block_kernel, half, taps, block), out_sh...]
    all_to_all x2 -> x0, starting transfers between devices: 10.1 us -> none  [the longest x1 6.35 us: on_device(): lax.all_to_all(by_channel, 'lon', split_axis=1, concat_axis=2, tiled=True)]
    gather x3 -> x0, local copies, waits for them, and re-layouts: 9.33 us -> none  [the longest x2 6.43 us: on_device(): to_slots = jnp.take(conv, dense_of_slot, axis=2) * slot_valid[None, None, :]]
    ppermute x2 -> x7, starting transfers between devices: 4.33 us -> 11.7 us  [the longest x2 5.68 us: to_near(): return lax.ppermute(value, 'lat', near_pairs)]
    all_to_all x3 -> x0, local copies, waits for them, and re-layouts: 6.4 us -> none  [the longest x2 4.74 us: on_device(): lax.all_to_all(to_slots, 'lon', split_axis=2, concat_axis=1, tiled=True)]
    unnamed x24 -> x0, local copies, waits for them, and re-layouts: 5.37 us -> none
  transfers between devices with their start and end apart: 4 -> 7, of which waited for: 2 -> 3; matrix products, arithmetic and copies ran while one was open for 8% -> 0% of each run, Pallas kernels for 0% -> 20%
where the time goes in v1:
time: 27.3 us; the launch traced here: 27 us
  starting transfers between devices  11.7 us (43%)
  Pallas kernels  10.5 us (38%)
  waiting for transfers between devices  4.8 us (18%)
    ppermute x2, starting transfers between devices, to_near(): return lax.ppermute(value, 'lat', near_pairs)  5.68 us
    pallas_call x1, Pallas kernels, on_device(): pl.pallas_call(functools.partial(block_kernel, half, taps, block), out_sh...  4.98 us
    ppermute x3, waiting for transfers between devices, on_device(): lax.ppermute(edges, 'lon', [(p, (p + step) % count) for p in range(count)])  4.79 us
    ppermute x3, starting transfers between devices, on_device(): lax.ppermute(edges, 'lon', [(p, (p + step) % count) for p in range(count)])  4.67 us
    pallas_call x1, Pallas kernels, on_device(): pl.pallas_call(functools.partial(own_kernel, half, block), out_shape=(vme...  3.16 us
    pallas_call x1, Pallas kernels, on_device(): pl.pallas_call(functools.partial(edges_kernel, half), out_shape=vmem_out(...  1.5 us
    ppermute x2, starting transfers between devices, to_far(): return lax.ppermute(value, 'lat', far_pairs)  1.37 us
    pallas_call x1, Pallas kernels, on_device(): pl.pallas_call(functools.partial(halo_kernel, count, half), out_shape=vme...  0.81 us
  transfers between devices with their start and end apart: 7, of which 3 were waited for; matrix products, arithmetic and copies ran while one was open for 0% of the time, Pallas kernels for 20%

profile of v1, /device:TPU:0, one launch (start us, length us, event | category | flops | bytes accessed | tf_op | source)
XLA Modules:
  0.0 27.0 jit_solution(13018416115037002971)
XLA Ops:
  0.0 0.7 %collective-permute-start.1 = (f32[360,640]{1,0:T(8,128)}, f32[360,640]{1,0:T(8,128)S(1)}, u32[]{:S(2)}, u32[]{:S(2)}) collective-permute-start(f32[360,640]{1,0:T(8,128)} %bitcast.2), channel_id=1, source_target_pairs={{1,2},{2,1},{5,6},{6,5},{9,10},{10,9},{13,14},{14,13},{17,18},{18,... | collective-permute-start | bytes 2764808 | tf_op jit(solution)/shard_map/ppermute | solution.py:224
  0.7 4.3 %collective-permute-start = (f32[360,640]{1,0:T(8,128)}, f32[360,640]{1,0:T(8,128)S(1)}, u32[]{:S(2)}, u32[]{:S(2)}) collective-permute-start(f32[360,640]{1,0:T(8,128)} %bitcast.3), channel_id=1, source_target_pairs={{0,1},{1,0},{2,3},{3,2},{4,5},{5,4},{6,7},{7,6},{8,9},{9,8},{10,11... | collective-permute-start | bytes 2764808 | tf_op jit(solution)/shard_map/ppermute | solution.py:221
  5.1 1.5 %edges.1 = f32[16,640]{1,0:T(8,128)S(1)} custom-call(s32[4]{0:T(128)} %lengths.7, f32[360,640]{1,0:T(8,128)} %bitcast.4), custom_call_target="tpu_custom_call" | custom-call | tf_op jit(solution)/shard_map/edges/pallas_call | solution.py:228
  6.6 3.7 %collective-permute-start.4 = (f32[16,640]{1,0:T(8,128)S(1)}, f32[16,640]{1,0:T(8,128)S(1)}, u32[]{:S(2)}, u32[]{:S(2)}) collective-permute-start(f32[16,640]{1,0:T(8,128)S(1)} %edges.1), channel_id=1, source_target_pairs={{0,12},{4,0},{8,4},{12,8},{1,13},{5,1},{9,5},{13,9},{2,14},{6,2},{... | collective-permute-start | bytes 122888 | tf_op jit(solution)/shard_map/ppermute | solution.py:241
  10.2 0.0 collective-permute-start.3
  10.2 1.0 %collective-permute-start.2 = (f32[16,640]{1,0:T(8,128)S(1)}, f32[16,640]{1,0:T(8,128)S(1)}, u32[]{:S(2)}, u32[]{:S(2)}) collective-permute-start(f32[16,640]{1,0:T(8,128)S(1)} %edges.1), channel_id=1, source_target_pairs={{0,4},{4,8},{8,12},{12,0},{1,5},{5,9},{9,13},{13,1},{2,6},{6,10},{... | collective-permute-start | bytes 122888 | tf_op jit(solution)/shard_map/ppermute | solution.py:241
  11.2 0.9 %collective-permute-done.4.refs_2_ = f32[16,640]{1,0:T(8,128)S(1)} collective-permute-done((f32[16,640]{1,0:T(8,128)S(1)}, f32[16,640]{1,0:T(8,128)S(1)}, u32[]{:S(2)}, u32[]{:S(2)}) %collective-permute-start.4) | collective-permute-done | bytes 40992 | tf_op jit(solution)/shard_map/ppermute | solution.py:241
  12.1 3.1 %collective-permute-done.3.refs_1_ = f32[16,640]{1,0:T(8,128)S(1)} collective-permute-done((f32[16,640]{1,0:T(8,128)S(1)}, f32[16,640]{1,0:T(8,128)S(1)}, u32[]{:S(2)}, u32[]{:S(2)}) %collective-permute-start.3) | collective-permute-done | bytes 40992 | tf_op jit(solution)/shard_map/ppermute | solution.py:241
  15.2 0.8 %collective-permute-done.2.refs_0_ = f32[16,640]{1,0:T(8,128)S(1)} collective-permute-done((f32[16,640]{1,0:T(8,128)S(1)}, f32[16,640]{1,0:T(8,128)S(1)}, u32[]{:S(2)}, u32[]{:S(2)}) %collective-permute-start.2) | collective-permute-done | bytes 40992 | tf_op jit(solution)/shard_map/ppermute | solution.py:241
  16.0 0.8 %halo.1.halos = f32[16,640]{1,0:T(8,128)S(1)} custom-call(s32[4]{0:T(128)} %lengths.7, f32[16,640]{1,0:T(8,128)S(1)} %collective-permute-done.2.refs_0_, f32[16,640]{1,0:T(8,128)S(1)} %collective-permute-done.3.refs_1_, f32[16,640]{1,0:T(8,128)S(1)} %collective-permute-done.4.refs_2_), custom_call_target="tpu_custom_call" | custom-call | tf_op jit(solution)/shard_map/halo/pallas_call | solution.py:243
  16.8 0.7 %collective-permute-start.6 = (f32[16,640]{1,0:T(8,128)S(1)}, f32[16,640]{1,0:T(8,128)S(1)}, u32[]{:S(2)}, u32[]{:S(2)}) collective-permute-start(f32[16,640]{1,0:T(8,128)S(1)} %halo.1.halos), channel_id=1, source_target_pairs={{1,2},{2,1},{5,6},{6,5},{9,10},{10,9},{13,14},{14,13},{17,18},{18,... | collective-permute-start | bytes 122888 | tf_op jit(solution)/shard_map/ppermute | solution.py:224
  17.5 1.3 %collective-permute-start.5 = (f32[16,640]{1,0:T(8,128)S(1)}, f32[16,640]{1,0:T(8,128)S(1)}, u32[]{:S(2)}, u32[]{:S(2)}) collective-permute-start(f32[16,640]{1,0:T(8,128)S(1)} %halo.1.halos), channel_id=1, source_target_pairs={{0,1},{1,0},{2,3},{3,2},{4,5},{5,4},{6,7},{7,6},{8,9},{9,8},{10,11... | collective-permute-start | bytes 122888 | tf_op jit(solution)/shard_map/ppermute | solution.py:221
  18.8 3.2 %own.1 = (f32[360,640]{1,0:T(8,128)S(1)}, f32[24,640]{1,0:T(8,128)S(1)}, f32[640]{0:T(1024)S(1)}, bf16[640,1280]{1,0:T(8,128)(2,1)S(1)}, f32[1280]{0:T(1024)S(1)...) custom-call(s32[4]{0:T(128)} %lengths.7, s32[4]{0:T(128)} %offsets.3, f32[9,4,2,17]{3,2,1,0:T(2,128)} %basis.1, ...), custom_call_target="tpu_custom_call" | custom-call | tf_op jit(solution)/shard_map/own/pallas_call | solution.py:255
  22.0 0.0 collective-permute-done.6.far_halo
  22.0 0.0 collective-permute-done.5.near_halo
  22.0 0.0 collective-permute-done.1.far
  22.0 0.0 collective-permute-done.near
  22.1 5.0 %block.1 = f32[360,640]{1,0:T(8,128)} custom-call(s32[4]{0:T(128)} %lengths.7, s32[4]{0:T(128)} %offsets.3, f32[360,640]{1,0:T(8,128)S(1)} %collective-permute-done.near, f32[360,640]{1,0:T(8,128)S(1)} %collective-permute-done.1.far, f32[16,640]{1,0:T(8,128)S(1)} %collective-permute-done.5.near_halo, f32[16,640]{1,0:T(8,128)S(1)} %collective-permute-done.6.far_halo, ...), custom_call_target="tpu_custom_call" | custom-call | tf_op jit(solution)/shard_map/block/pallas_call | solution.py:274
Async XLA Ops:
  0.0 22.0 %collective-permute-start.1 = (f32[360,640]{1,0:T(8,128)}, f32[360,640]{1,0:T(8,128)S(1)}, u32[]{:S(2)}, u32[]{:S(2)}) collective-permute-start(f32[360,640]{1,0:T(8,128)} %bitcast.2), channel_id=1, source_target_pairs={{1,2},{2,1},{5,6},{6,5},{9,10},{10,9},{13,14},{14,13},{17,18},{18,... | collective-permute-start | bytes 2764808 | tf_op jit(solution)/shard_map/ppermute | solution.py:224
  0.7 21.3 %collective-permute-start = (f32[360,640]{1,0:T(8,128)}, f32[360,640]{1,0:T(8,128)S(1)}, u32[]{:S(2)}, u32[]{:S(2)}) collective-permute-start(f32[360,640]{1,0:T(8,128)} %bitcast.3), channel_id=1, source_target_pairs={{0,1},{1,0},{2,3},{3,2},{4,5},{5,4},{6,7},{7,6},{8,9},{9,8},{10,11... | collective-permute-start | bytes 2764808 | tf_op jit(solution)/shard_map/ppermute | solution.py:221
  6.6 5.6 %collective-permute-start.4 = (f32[16,640]{1,0:T(8,128)S(1)}, f32[16,640]{1,0:T(8,128)S(1)}, u32[]{:S(2)}, u32[]{:S(2)}) collective-permute-start(f32[16,640]{1,0:T(8,128)S(1)} %edges.1), channel_id=1, source_target_pairs={{0,12},{4,0},{8,4},{12,8},{1,13},{5,1},{9,5},{13,9},{2,14},{6,2},{... | collective-permute-start | bytes 122888 | tf_op jit(solution)/shard_map/ppermute | solution.py:241
  10.2 5.0 %collective-permute-start.3 = (f32[16,640]{1,0:T(8,128)S(1)}, f32[16,640]{1,0:T(8,128)S(1)}, u32[]{:S(2)}, u32[]{:S(2)}) collective-permute-start(f32[16,640]{1,0:T(8,128)S(1)} %edges.1), channel_id=1, source_target_pairs={{0,8},{4,12},{8,0},{12,4},{1,9},{5,13},{9,1},{13,5},{2,10},{6,14},... | collective-permute-start | bytes 122888 | tf_op jit(solution)/shard_map/ppermute | solution.py:241
  10.2 5.8 %collective-permute-start.2 = (f32[16,640]{1,0:T(8,128)S(1)}, f32[16,640]{1,0:T(8,128)S(1)}, u32[]{:S(2)}, u32[]{:S(2)}) collective-permute-start(f32[16,640]{1,0:T(8,128)S(1)} %edges.1), channel_id=1, source_target_pairs={{0,4},{4,8},{8,12},{12,0},{1,5},{5,9},{9,13},{13,1},{2,6},{6,10},{... | collective-permute-start | bytes 122888 | tf_op jit(solution)/shard_map/ppermute | solution.py:241
  16.8 5.2 %collective-permute-start.6 = (f32[16,640]{1,0:T(8,128)S(1)}, f32[16,640]{1,0:T(8,128)S(1)}, u32[]{:S(2)}, u32[]{:S(2)}) collective-permute-start(f32[16,640]{1,0:T(8,128)S(1)} %halo.1.halos), channel_id=1, source_target_pairs={{1,2},{2,1},{5,6},{6,5},{9,10},{10,9},{13,14},{14,13},{17,18},{18,... | collective-permute-start | bytes 122888 | tf_op jit(solution)/shard_map/ppermute | solution.py:224
  17.5 4.5 %collective-permute-start.5 = (f32[16,640]{1,0:T(8,128)S(1)}, f32[16,640]{1,0:T(8,128)S(1)}, u32[]{:S(2)}, u32[]{:S(2)}) collective-permute-start(f32[16,640]{1,0:T(8,128)S(1)} %halo.1.halos), channel_id=1, source_target_pairs={{0,1},{1,0},{2,3},{3,2},{4,5},{5,4},{6,7},{7,6},{8,9},{9,8},{10,11... | collective-permute-start | bytes 122888 | tf_op jit(solution)/shard_map/ppermute | solution.py:221

commit v2 on v1

v2 whole, which is shorter than its diff:
```python
import functools

import jax
import jax.numpy as jnp
from jax import lax
from jax.experimental import pallas as pl
from jax.experimental.pallas import tpu as pltpu
from jax.sharding import PartitionSpec as P

LANES = 128
META = 8
HBM = pl.BlockSpec(memory_space=pltpu.HBM)
SMEM = pl.BlockSpec(memory_space=pltpu.SMEM)
VMEM = pl.BlockSpec(memory_space=pltpu.VMEM)


def up8(value):
    return (value + 7) // 8 * 8


def in_vmem(value):
    return pltpu.with_memory_space_constraint(value, pltpu.VMEM)


def in_hbm(value):
    return pltpu.with_memory_space_constraint(value, pltpu.HBM)


def grant(mib):
    return pltpu.CompilerParams(vmem_limit_bytes=mib << 20)


def vmem_out(shape, dtype=jnp.float32):
    return pltpu.VMEM(shape, dtype)


def load_kernel(count, half, lengths, offsets, own, edges, window, meta, rows, sem):
    me, lat = lax.axis_index("lon"), lax.axis_index("lat")
    columns, cap = window.shape[0], own.shape[0]
    length = lengths[me]
    at = lat - offsets[lat]
    if cap % 8 == 0:
        copies = [
            pltpu.make_async_copy(
                own.at[:, pl.ds(column * LANES, LANES)], window.at[column, pl.ds(half, cap), :], sem
            )
            for column in range(columns)
        ]
    else:
        copies = [pltpu.make_async_copy(own, rows, sem)]
    for copy in copies:
        copy.start()
    meta[0], meta[1], meta[2] = length, at, 1 - lax.rem(at + lat, 2)
    halo_rows(count, half, me, lengths, meta)
    for copy in copies:
        copy.wait()
    zeros = jnp.zeros((half, LANES), jnp.float32)
    last = jnp.maximum(length - half, 0)
    for column in range(columns):
        lanes = pl.ds(column * LANES, LANES)
        if cap % 8:
            window[column, pl.ds(half, cap), :] = rows[:, lanes]
        window[column, pl.ds(0, half), :] = zeros
        edges[pl.ds(0, half), lanes] = window[column, pl.ds(half, half), :]
        edges[pl.ds(half, half), lanes] = window[column, pl.ds(half + last, half), :]
    for column in range(columns):
        window[column, pl.ds(half + length, half), :] = zeros


def halo_rows(count, half, me, lengths, meta):
    def row_of(piece, row):
        return (lax.rem(me - piece + count, count) - 1) * (2 * half) + row

    piece = lax.rem(me + count - 1, count)
    slot = lengths[piece] - 1
    for near in range(1, half + 1):
        meta[META + half - near] = row_of(piece, half + slot - jnp.maximum(lengths[piece] - half, 0))
        before = lax.rem(piece + count - 1, count)
        piece, slot = (
            jnp.where(slot > 0, piece, before),
            jnp.where(slot > 0, slot - 1, lengths[before] - 1),
        )
    piece = lax.rem(me + 1, count)
    slot = jnp.int32(0)
    for near in range(half):
        meta[META + half + near] = row_of(piece, slot)
        inside = slot + 1 < lengths[piece]
        piece, slot = (
            jnp.where(inside, piece, lax.rem(piece + 1, count)),
            jnp.where(inside, slot + 1, 0),
        )


def halo_kernel(half, meta, *refs):
    received, out, stack = refs[:-2], refs[-2], refs[-1]
    for step, ref in enumerate(received):
        stack[pl.ds(step * 2 * half, 2 * half), :] = ref[...]
    for row in range(2 * half):
        out[pl.ds(row, 1), :] = stack[pl.ds(meta[META + row], 1), :]


def fill_window(window, rows, halos, half, length):
    cap = rows.shape[0]
    for column in range(window.shape[0]):
        lanes = pl.ds(column * LANES, LANES)
        window[column, pl.ds(0, half), :] = halos[pl.ds(0, half), lanes]
        window[column, pl.ds(half, cap), :] = rows[:, lanes]
    for column in range(window.shape[0]):
        lanes = pl.ds(column * LANES, LANES)
        window[column, pl.ds(half + length, half), :] = halos[pl.ds(half, half), lanes]


def add_own_halos(partial, halos, coef, edge, half, length, taps):
    columns = partial.shape[0]
    zeros = jnp.zeros((half, LANES), jnp.float32)
    for side, (at, to) in enumerate(((0, half), (2 * half, length))):
        for column in range(columns):
            for part in range(3):
                edge[side, column, pl.ds(part * half, half), :] = zeros
            edge[side, column, pl.ds(at, half), :] = halos[pl.ds(side * half, half), pl.ds(column * LANES, LANES)]
        for column in range(columns):
            here = pl.ds(to, half)
            partial[column, here, :] = add_taps(
                partial[column, here, :], edge.at[side], column, 0, half, coef, taps
            )


def add_taps(total, window, column, first, rows, coef, taps):
    lanes = pl.ds(column * LANES, LANES)
    for phase in range(min(8, taps)):
        steps = (taps - phase + 7) // 8
        block = window[column, pl.ds(first + phase, rows + 8 * (steps - 1)), :]
        for step in range(steps):
            weight = coef[pl.ds(8 * step + phase, 1), lanes]
            total = total + weight * block[8 * step : 8 * step + rows]
    return total


def own_rows(half, block, lower, upper, window, coef, taps, out):
    for first in range(lower, upper, block):
        rows = min(block, upper - first)
        for column in range(window.shape[0]):
            state = window[column, pl.ds(half + first, rows), :]
            out[column, pl.ds(half + first, rows), :] = add_taps(state, window, column, first, rows, coef, taps)


def own_kernel(half, block, split, meta, basis, depth_weight, window, *refs):
    lat = lax.axis_index("lat")
    held = (len(refs) - 4) // 2
    sources, out, coef_own, coef_other = refs[:held], *refs[held : held + 3]
    copied, sem = refs[held + 3 : 2 * held + 3], refs[2 * held + 3]
    copies = [pltpu.make_async_copy(a, b, sem) for a, b in zip(sources, copied)]
    for copy in copies:
        copy.start()
    at = meta[1]
    taps = basis.shape[3]
    for which, ref in ((at, coef_own), (1 - at, coef_other)):
        ref[pl.ds(0, taps), :] = lax.dot_general(
            basis[:, lat, which, :],
            depth_weight[...],
            (((0,), (0,)), ((), ())),
            precision=lax.Precision.HIGHEST,
            preferred_element_type=jnp.float32,
        )
    own_rows(half, block, 0, split, window, coef_own, taps, out)
    for copy in copies:
        copy.wait()


def rest_kernel(half, taps, block, split, upper, meta, window, coef_own, halos, _, out, edge):
    own_rows(half, block, split, upper, window, coef_own, taps, out)
    add_own_halos(out, halos, coef_own, edge, half, meta[0], taps)


def block_kernel(half, taps, block, meta, near, far, near_halo, far_halo, partial, coef, gain,
                 w_in, b_in, w_out, b_out, out, window, state, normed, hidden, result, sem):
    length = meta[0]
    columns = window.shape[0]
    width = columns * LANES
    cap = near.shape[0]
    rows_all = state.shape[0]

    @pl.when(meta[2] == 1)
    def _():
        fill_window(window, near, near_halo, half, length)

    @pl.when(meta[2] == 0)
    def _():
        fill_window(window, far, far_halo, half, length)

    for first in range(0, rows_all, block):
        rows = min(block, rows_all - first)
        here = pl.ds(first, rows)
        for column in range(columns):
            state[here, pl.ds(column * LANES, LANES)] = add_taps(
                partial[column, pl.ds(half + first, rows), :], window, column, first, rows, coef, taps
            )
    for first in range(0, rows_all, 72):
        rows = min(72, rows_all - first)
        here = pl.ds(first, rows)
        value = state[here, :]
        scale = lax.rsqrt(jnp.sum(value * value, axis=1, keepdims=True) / width + 1e-05)
        normed[here, :] = (value * scale * gain[...][None, :]).astype(jnp.bfloat16)
    step = 256
    for start in range(0, w_in.shape[1], step):
        part = pl.ds(start, step)
        pre = jnp.dot(normed[...], w_in[:, part], preferred_element_type=jnp.float32)
        pre = pre + b_in[part][None, :]
        active = 0.5 * pre * (1.0 + lax.erf(pre * 0.7071067811865476))
        hidden[:, part] = active.astype(jnp.bfloat16)
    inside = lax.broadcasted_iota(jnp.int32, (rows_all, 1), 0) < length
    copies = []
    for start in range(0, width, step):
        part = pl.ds(start, min(step, width - start))
        mixed = jnp.dot(hidden[...], w_out[:, part], preferred_element_type=jnp.float32)
        value = jnp.where(inside, state[:, part] + (mixed + b_out[part][None, :]), 0.0)
        result[:, part] = value[:cap]
        copy = pltpu.make_async_copy(result.at[:, part], out.at[:, part], sem)
        copy.start()
        copies.append(copy)
    for copy in copies:
        copy.wait()


def on_device(field, piece_lengths, offsets, basis, depth_weight, gain, w_in, b_in, w_out, b_out):
    _, cap, channels = field.shape
    count = lax.axis_size("lon")
    lats = lax.axis_size("lat")
    taps = basis.shape[3]
    half = taps // 2
    columns = channels // LANES
    cap8 = up8(cap)
    hid = w_in.shape[1]
    block = 120

    own = in_hbm(field.reshape(cap, channels))
    piece_lengths, offsets = in_hbm(piece_lengths), in_hbm(offsets)
    near_pairs = [(a, a ^ 1) for a in range(lats) if (a ^ 1) < lats]
    far_pairs = [(a, a + 1) for a in range(1, lats - 1, 2)] + [(a + 1, a) for a in range(1, lats - 1, 2)]

    def to_near(value):
        return lax.ppermute(value, "lat", near_pairs)

    parts = lax.axis_size("ens")
    far_full = [(e * lats + a, e * lats + b) for e in range(parts) for a, b in far_pairs]
    far_full += [(e * lats + a, (e + 1) % parts * lats + a) for e in range(parts) for a in (0, lats - 1)]

    def to_far(value):
        return lax.ppermute(value, ("ens", "lat"), far_full)

    far = to_far(own)
    near = to_near(own)
    padded = (columns, cap8 + 2 * half + 16, LANES)
    edges, window, meta = pl.pallas_call(
        functools.partial(load_kernel, count, half),
        out_shape=(
            vmem_out((2 * half, channels)),
            vmem_out(padded),
            pltpu.SMEM((META + 2 * half,), jnp.int32),
        ),
        in_specs=[SMEM, SMEM, HBM],
        out_specs=(VMEM, VMEM, SMEM),
        scratch_shapes=[
            pltpu.VMEM((8 if cap % 8 == 0 else cap, channels), jnp.float32),
            pltpu.SemaphoreType.DMA,
        ],
        compiler_params=grant(8),
        name="load",
    )(piece_lengths, offsets, own)
    received = [
        lax.ppermute(edges, "lon", [(p, (p + step) % count) for p in range(count)]) for step in range(1, count)
    ]
    operands = (gain, w_in, b_in, w_out, b_out)
    split = min(120, cap8)
    partial, coef_own, coef, *operands = pl.pallas_call(
        functools.partial(own_kernel, half, block, split),
        out_shape=(
            vmem_out(padded),
            vmem_out((up8(taps), channels)),
            vmem_out((up8(taps), channels)),
            *[vmem_out(value.shape, value.dtype) for value in operands],
        ),
        in_specs=[SMEM, VMEM, VMEM, VMEM] + [HBM] * len(operands),
        out_specs=(VMEM,) * (3 + len(operands)),
        scratch_shapes=[pltpu.SemaphoreType.DMA],
        compiler_params=grant(8),
        name="own",
    )(meta, in_hbm(basis), in_hbm(depth_weight), window, *[in_hbm(v) for v in operands])
    partial, *held = lax.optimization_barrier((partial, *received))
    halos = pl.pallas_call(
        functools.partial(halo_kernel, half),
        out_shape=vmem_out((2 * half, channels)),
        in_specs=[SMEM] + [VMEM] * len(held),
        out_specs=VMEM,
        scratch_shapes=[pltpu.VMEM((max(1, count - 1) * 2 * half, channels), jnp.float32)],
        compiler_params=grant(8),
        name="halo",
    )(meta, *[in_vmem(r) for r in held])
    near_halo, far_halo = to_near(halos), to_far(halos)
    partial = pl.pallas_call(
        functools.partial(rest_kernel, half, taps, block, split, cap8),
        out_shape=vmem_out(padded),
        in_specs=[SMEM, VMEM, VMEM, VMEM, VMEM],
        out_specs=VMEM,
        scratch_shapes=[pltpu.VMEM((2, columns, 3 * half, LANES), jnp.float32)],
        input_output_aliases={4: 0},
        compiler_params=grant(8),
        name="rest",
    )(meta, window, coef_own, halos, partial)
    out = pl.pallas_call(
        functools.partial(block_kernel, half, taps, block),
        out_shape=jax.ShapeDtypeStruct((cap, channels), jnp.float32),
        in_specs=[SMEM] + [VMEM] * 11,
        out_specs=HBM,
        scratch_shapes=[
            pltpu.VMEM(padded, jnp.float32),
            pltpu.VMEM((cap8, channels), jnp.float32),
            pltpu.VMEM((cap8, channels), jnp.bfloat16),
            pltpu.VMEM((cap8, hid), jnp.bfloat16),
            pltpu.VMEM((cap, channels), jnp.float32),
            pltpu.SemaphoreType.DMA,
        ],
        compiler_params=grant(24),
        name="block",
    )(meta, in_vmem(near), in_vmem(far), in_vmem(near_halo), in_vmem(far_halo), partial, coef, *operands)
    return out.reshape(1, cap, channels)


def solution(mesh):
    placed = (P(("ens", "lat"), "lon", None), P(), P(), P(), P(), P(), P(), P(), P(), P())
    return jax.shard_map(
        on_device,
        mesh=mesh,
        in_specs=placed,
        out_specs=P(("ens", "lat"), "lon", None),
        check_vma=False,
    )
```

time: 27.3 us -> 22.2 us (0.81)
  starting transfers between devices: 11.7 us -> 9.39 us
  waiting for transfers between devices: 4.8 us -> 2.53 us
  Pallas kernels: 10.5 us -> 9.98 us
    ppermute x2, starting transfers between devices: 5.68 us -> 0.56 us  [to_near(): return lax.ppermute(value, 'lat', near_pairs)]
    ppermute x3, waiting for transfers between devices: 4.79 us -> 0.01 us  [on_device(): lax.ppermute(edges, 'lon', [(p, (p + step) % count) for p in range(count)])]
    ppermute x2, waiting for transfers between devices: 0.01 us -> 2.52 us  [to_far(): return lax.ppermute(value, ('ens', 'lat'), far_full)]
    ppermute x2, starting transfers between devices: 1.37 us -> 3.26 us  [to_far(): return lax.ppermute(value, ('ens', 'lat'), far_full)]
    ppermute x3, starting transfers between devices: 4.67 us -> 5.57 us  [on_device(): lax.ppermute(edges, 'lon', [(p, (p + step) % count) for p in range(count)])]
    pallas_call x1, Pallas kernels: 4.98 us -> 4.43 us  [on_device(): pl.pallas_call(functools.partial(block_kernel, half, taps, block), out_sh...]
    pallas_call x3 -> x4, Pallas kernels: 5.47 us -> 5.55 us  [the longest x1 2.77 us: on_device(): pl.pallas_call(functools.partial(own_kernel, half, block, split), out_sha...]
  transfers between devices with their start and end apart: 7 -> 7, of which waited for: 3 -> 1; matrix products, arithmetic and copies ran while one was open for 0% -> 0% of each run, Pallas kernels for 20% -> 25%
where the time goes in v2:
time: 22.2 us; the launch traced here: 22 us
  Pallas kernels  9.98 us (45%)
  starting transfers between devices  9.39 us (42%)
  waiting for transfers between devices  2.53 us (11%)
    ppermute x3, starting transfers between devices, on_device(): lax.ppermute(edges, 'lon', [(p, (p + step) % count) for p in range(count)])  5.57 us
    pallas_call x1, Pallas kernels, on_device(): pl.pallas_call(functools.partial(block_kernel, half, taps, block), out_sh...  4.43 us
    ppermute x2, starting transfers between devices, to_far(): return lax.ppermute(value, ('ens', 'lat'), far_full)  3.26 us
    pallas_call x1, Pallas kernels, on_device(): pl.pallas_call(functools.partial(own_kernel, half, block, split), out_sha...  2.77 us
    ppermute x2, waiting for transfers between devices, to_far(): return lax.ppermute(value, ('ens', 'lat'), far_full)  2.52 us
    pallas_call x1, Pallas kernels, on_device(): pl.pallas_call(functools.partial(load_kernel, count, half), out_shape=(vm...  1.95 us
    pallas_call x1, Pallas kernels, on_device(): pl.pallas_call(functools.partial(rest_kernel, half, taps, block, split, c...  0.78 us
    ppermute x2, starting transfers between devices, to_near(): return lax.ppermute(value, 'lat', near_pairs)  0.56 us
  transfers between devices with their start and end apart: 7, of which 1 were waited for; matrix products, arithmetic and copies ran while one was open for 0% of the time, Pallas kernels for 25%

profile of v2, /device:TPU:0, one launch (start us, length us, event | category | flops | bytes accessed | tf_op | source)
XLA Modules:
  0.0 22.0 jit_solution(12885641276489470924)
XLA Ops:
  0.0 0.5 %collective-permute-start = (f32[360,640]{1,0:T(8,128)}, f32[360,640]{1,0:T(8,128)S(1)}, u32[]{:S(2)}, u32[]{:S(2)}) collective-permute-start(f32[360,640]{1,0:T(8,128)} %bitcast.2), channel_id=1, source_target_pairs={{0,1},{1,0},{2,3},{3,2},{4,5},{5,4},{6,7},{7,6},{8,9},{9,8},{10,11... | collective-permute-start | bytes 2764808 | tf_op jit(solution)/shard_map/ppermute | solution.py:242
  0.5 2.5 %collective-permute-start.1 = (f32[360,640]{1,0:T(8,128)}, f32[360,640]{1,0:T(8,128)S(1)}, u32[]{:S(2)}, u32[]{:S(2)}) collective-permute-start(f32[360,640]{1,0:T(8,128)} %bitcast.3), channel_id=1, source_target_pairs={{1,2},{2,1},{17,18},{18,17},{0,16},{3,19},{16,0},{19,3},{5,6},{6,5... | collective-permute-start | bytes 2764808 | tf_op jit(solution)/shard_map/ppermute | solution.py:249
  3.0 2.0 %load.1 = (f32[16,640]{1,0:T(8,128)S(1)}, f32[5,392,128]{2,1,0:T(8,128)S(1)}, s32[24]{0:T(128)S(4)}) custom-call(s32[4]{0:T(128)} %lengths.1, s32[4]{0:T(128)} %offsets.1, f32[360,640]{1,0:T(8,128)} %bitcast.4), custom_call_target="tpu_custom_call" | custom-call | tf_op jit(solution)/shard_map/load/pallas_call | solution.py:254
  5.0 1.6 %collective-permute-start.2 = (f32[16,640]{1,0:T(8,128)S(1)}, f32[16,640]{1,0:T(8,128)S(1)}, u32[]{:S(2)}, u32[]{:S(2)}) collective-permute-start(f32[16,640]{1,0:T(8,128)S(1)} %get-tuple-element.23), channel_id=1, source_target_pairs={{0,4},{4,8},{8,12},{12,0},{1,5},{5,9},{9,13},{13,1},{2,6},{6,10},{... | collective-permute-start | bytes 122888 | tf_op jit(solution)/shard_map/ppermute | solution.py:271
  6.6 2.6 %collective-permute-start.3 = (f32[16,640]{1,0:T(8,128)S(1)}, f32[16,640]{1,0:T(8,128)S(1)}, u32[]{:S(2)}, u32[]{:S(2)}) collective-permute-start(f32[16,640]{1,0:T(8,128)S(1)} %get-tuple-element.23), channel_id=1, source_target_pairs={{0,8},{4,12},{8,0},{12,4},{1,9},{5,13},{9,1},{13,5},{2,10},{6,14},... | collective-permute-start | bytes 122888 | tf_op jit(solution)/shard_map/ppermute | solution.py:271
  9.2 1.3 %collective-permute-start.4 = (f32[16,640]{1,0:T(8,128)S(1)}, f32[16,640]{1,0:T(8,128)S(1)}, u32[]{:S(2)}, u32[]{:S(2)}) collective-permute-start(f32[16,640]{1,0:T(8,128)S(1)} %get-tuple-element.23), channel_id=1, source_target_pairs={{0,12},{4,0},{8,4},{12,8},{1,13},{5,1},{9,5},{13,9},{2,14},{6,2},{... | collective-permute-start | bytes 122888 | tf_op jit(solution)/shard_map/ppermute | solution.py:271
  10.5 2.8 %own.1 = (f32[5,392,128]{2,1,0:T(8,128)S(1)}, f32[24,640]{1,0:T(8,128)S(1)}, f32[24,640]{1,0:T(8,128)S(1)}, f32[640]{0:T(1024)S(1)}, bf16[640,1280]{1,0:T(8,128)...) custom-call(s32[24]{0:T(128)S(4)} %get-tuple-element.20.meta, f32[9,4,2,17]{3,2,1,0:T(2,128)} %basis.1, ...), custom_call_target="tpu_custom_call" | custom-call | tf_op jit(solution)/shard_map/own/pallas_call | solution.py:275
  13.3 0.0 collective-permute-done.2.refs_0_
  13.3 0.0 collective-permute-done.3.refs_1_
  13.3 0.0 collective-permute-done.4.refs_2_
  13.4 0.1 collective-permute-start.5
  13.5 0.8 %collective-permute-start.6 = (f32[16,640]{1,0:T(8,128)S(1)}, f32[16,640]{1,0:T(8,128)S(1)}, u32[]{:S(2)}, u32[]{:S(2)}) collective-permute-start(f32[16,640]{1,0:T(8,128)S(1)} %halo.1.halos), channel_id=1, source_target_pairs={{1,2},{2,1},{17,18},{18,17},{0,16},{3,19},{16,0},{19,3},{5,6},{6,5... | collective-permute-start | bytes 122888 | tf_op jit(solution)/shard_map/ppermute | solution.py:249
  14.2 0.8 %rest.1.partial = f32[5,392,128]{2,1,0:T(8,128)S(1)} custom-call(s32[24]{0:T(128)S(4)} %get-tuple-element.20.meta, f32[5,392,128]{2,1,0:T(8,128)S(1)} %get-tuple-element.21.window, f32[24,640]{1,0:T(8,128)S(1)} %get-tuple-element.27.coef_own, f32[16,640]{1,0:T(8,128)S(1)} %halo.1.halos, ...), custom_call_target="tpu_custom_call", output_to_operand_aliasing={{}: (4, {})} | custom-call | tf_op jit(solution)/shard_map/rest/pallas_call | solution.py:300
  15.0 0.0 collective-permute-done.5.near_halo
  15.0 2.5 %collective-permute-done.6.far_halo = f32[16,640]{1,0:T(8,128)S(1)} collective-permute-done((f32[16,640]{1,0:T(8,128)S(1)}, f32[16,640]{1,0:T(8,128)S(1)}, u32[]{:S(2)}, u32[]{:S(2)}) %collective-permute-start.6) | collective-permute-done | bytes 40992 | tf_op jit(solution)/shard_map/ppermute | solution.py:249
  17.5 0.0 collective-permute-done.near
  17.5 0.0 collective-permute-done.1.far
  17.5 4.4 %block.1 = f32[360,640]{1,0:T(8,128)} custom-call(s32[24]{0:T(128)S(4)} %get-tuple-element.20.meta, f32[360,640]{1,0:T(8,128)S(1)} %collective-permute-done.near, f32[360,640]{1,0:T(8,128)S(1)} %collective-permute-done.1.far, f32[16,640]{1,0:T(8,128)S(1)} %collective-permute-done.5.near_halo, f32[16,640]{1,0:T(8,128)S(1)} %collective-permute-done.6.far_halo, ...), custom_call_target="tpu_custom_call" | custom-call | tf_op jit(solution)/shard_map/block/pallas_call | solution.py:310
  (1 shorter events, 0.0 us)
Async XLA Ops:
  0.0 17.5 %collective-permute-start = (f32[360,640]{1,0:T(8,128)}, f32[360,640]{1,0:T(8,128)S(1)}, u32[]{:S(2)}, u32[]{:S(2)}) collective-permute-start(f32[360,640]{1,0:T(8,128)} %bitcast.2), channel_id=1, source_target_pairs={{0,1},{1,0},{2,3},{3,2},{4,5},{5,4},{6,7},{7,6},{8,9},{9,8},{10,11... | collective-permute-start | bytes 2764808 | tf_op jit(solution)/shard_map/ppermute | solution.py:242
  0.5 17.0 %collective-permute-start.1 = (f32[360,640]{1,0:T(8,128)}, f32[360,640]{1,0:T(8,128)S(1)}, u32[]{:S(2)}, u32[]{:S(2)}) collective-permute-start(f32[360,640]{1,0:T(8,128)} %bitcast.3), channel_id=1, source_target_pairs={{1,2},{2,1},{17,18},{18,17},{0,16},{3,19},{16,0},{19,3},{5,6},{6,5... | collective-permute-start | bytes 2764808 | tf_op jit(solution)/shard_map/ppermute | solution.py:249
  5.0 8.3 %collective-permute-start.2 = (f32[16,640]{1,0:T(8,128)S(1)}, f32[16,640]{1,0:T(8,128)S(1)}, u32[]{:S(2)}, u32[]{:S(2)}) collective-permute-start(f32[16,640]{1,0:T(8,128)S(1)} %get-tuple-element.23), channel_id=1, source_target_pairs={{0,4},{4,8},{8,12},{12,0},{1,5},{5,9},{9,13},{13,1},{2,6},{6,10},{... | collective-permute-start | bytes 122888 | tf_op jit(solution)/shard_map/ppermute | solution.py:271
  6.6 6.7 %collective-permute-start.3 = (f32[16,640]{1,0:T(8,128)S(1)}, f32[16,640]{1,0:T(8,128)S(1)}, u32[]{:S(2)}, u32[]{:S(2)}) collective-permute-start(f32[16,640]{1,0:T(8,128)S(1)} %get-tuple-element.23), channel_id=1, source_target_pairs={{0,8},{4,12},{8,0},{12,4},{1,9},{5,13},{9,1},{13,5},{2,10},{6,14},... | collective-permute-start | bytes 122888 | tf_op jit(solution)/shard_map/ppermute | solution.py:271
  9.2 4.1 %collective-permute-start.4 = (f32[16,640]{1,0:T(8,128)S(1)}, f32[16,640]{1,0:T(8,128)S(1)}, u32[]{:S(2)}, u32[]{:S(2)}) collective-permute-start(f32[16,640]{1,0:T(8,128)S(1)} %get-tuple-element.23), channel_id=1, source_target_pairs={{0,12},{4,0},{8,4},{12,8},{1,13},{5,1},{9,5},{13,9},{2,14},{6,2},{... | collective-permute-start | bytes 122888 | tf_op jit(solution)/shard_map/ppermute | solution.py:271
  13.4 1.6 %collective-permute-start.5 = (f32[16,640]{1,0:T(8,128)S(1)}, f32[16,640]{1,0:T(8,128)S(1)}, u32[]{:S(2)}, u32[]{:S(2)}) collective-permute-start(f32[16,640]{1,0:T(8,128)S(1)} %halo.1.halos), channel_id=1, source_target_pairs={{0,1},{1,0},{2,3},{3,2},{4,5},{5,4},{6,7},{7,6},{8,9},{9,8},{10,11... | collective-permute-start | bytes 122888 | tf_op jit(solution)/shard_map/ppermute | solution.py:242
  13.5 4.1 %collective-permute-start.6 = (f32[16,640]{1,0:T(8,128)S(1)}, f32[16,640]{1,0:T(8,128)S(1)}, u32[]{:S(2)}, u32[]{:S(2)}) collective-permute-start(f32[16,640]{1,0:T(8,128)S(1)} %halo.1.halos), channel_id=1, source_target_pairs={{1,2},{2,1},{17,18},{18,17},{0,16},{3,19},{16,0},{19,3},{5,6},{6,5... | collective-permute-start | bytes 122888 | tf_op jit(solution)/shard_map/ppermute | solution.py:249
